TPU v7x, 32 devices: a whole 2x2x4 slice. The times are simulated.
32 devices in a mesh: dp: 8 (over z, x), mp: 4 (over y, core).
Axes of the slice: x: 2, y: 2, z: 4, core: 2. Of those that a mesh axis runs over, the one named last changes fastest.
Arguments:
- tokens: bfloat16 [256, 48, 3584], P('dp', None, 'mp'), may hold values from -180 to 180
- norm_gain: float32 [3584], replicated, may hold values from 0.1 to 1.9
- w_query: bfloat16 [3584, 3584], P('dp', 'mp'), may hold values from -0.16 to 0.16
- w_keyval: bfloat16 [3584, 2, 512], P('dp', None, 'mp'), may hold values from -0.16 to 0.16
- w_out: bfloat16 [3584, 3584], P('mp', 'dp'), may hold values from -0.09375 to 0.09375
- residents: bfloat16 [8, 2048, 3584], P('dp', 'mp'), may hold values from -6 to 6
- lengths: int32 [256], P('dp'), may hold values from 6 to 48
- cluster: int32 [256, 1], P('dp'), may hold values from 0 to 7; in each aligned block of 32 rows (0 to 31, 32 to 63, ...) at most 4 rows name the same one
- owner: int32 [8], replicated, may hold values from 0 to 7, each once
- counts: int32 [8], replicated, may hold values from 256 to 2048
- flags: int32 [256], P('dp'), may hold values 0 or 1
Outputs:
- similarity: float32 [256, 2048], P('dp', 'mp')
Inputs may be any that keep to these rules, and one draw needn't show every extreme that they name: Each dialogue's cluster; among the 32 dialogues of one index of dp (aligned blocks of rows) no cluster is named more than 4 times. owner gives every cluster a distinct index of dp that holds its residents.
All inputs are finite; a program needn't handle non-finite values. No bound on the sum of `flags` on one device may be relied on, other than what follows from the above.
Results may differ from a plain program's by a relative error of at most 0.013.
Values may be sent and summed in bfloat16 or wider, within the bound.
A program may use at most 128 MiB of HBM per device.

v0:
```python
import math
import jax
import jax.numpy as jnp
from jax import lax
from jax.sharding import PartitionSpec as P

HEAD_DIM = 128
rope_base = 1000000.0
logit_scale = 100.0


def rotate(values, positions):
    half = values.shape[-1] // 2
    freqs = rope_base ** (-jnp.arange(half, dtype=jnp.float32) * 2.0 / values.shape[-1])
    angles = positions.astype(jnp.float32)[:, None] * freqs[None, :]
    cosine = jnp.cos(angles)[:, None, :]
    sine = jnp.sin(angles)[:, None, :]
    first = values[..., :half]
    second = values[..., half:]
    return jnp.concatenate(
        [first * cosine - second * sine, second * cosine + first * sine], axis=-1
    )


def attend(query, keys, values, length):
    seq_len = query.shape[0]
    kv_count = keys.shape[1]
    group = query.shape[1] // kv_count
    grouped = query.reshape(seq_len, kv_count, group, query.shape[-1])
    scores = jnp.einsum(
        "qkgd,pkd->kgqp", grouped, keys, preferred_element_type=jnp.float32
    ) / math.sqrt(query.shape[-1])
    row_pos = jnp.arange(seq_len)[:, None]
    col_pos = jnp.arange(seq_len)[None, :]
    allowed = (col_pos <= row_pos) & (col_pos < length)
    scores = jnp.where(allowed, scores, -1e30)
    highest = jnp.max(scores, axis=-1, keepdims=True)
    expanded = jnp.exp(scores - highest)
    weights = (expanded / jnp.sum(expanded, axis=-1, keepdims=True)).astype(jnp.bfloat16)
    context = jnp.einsum("kgqp,pkd->qkgd", weights, values, preferred_element_type=jnp.float32)
    valid = (jnp.arange(seq_len) < length).astype(jnp.float32)
    pooled = jnp.sum(context * valid[:, None, None, None], axis=0) / length.astype(jnp.float32)
    return pooled.reshape(-1)


def local(
    tokens, norm_gain, w_query, w_keyval, w_out, residents, lengths, cluster, owner, counts, flags
):
    gathered = lax.all_gather(tokens, "mp", axis=2, tiled=True)
    dialogs, seq_len, width = gathered.shape
    hidden = gathered.astype(jnp.float32)
    normed = (
        hidden * lax.rsqrt(jnp.mean(hidden * hidden, axis=-1, keepdims=True) + 1e-06) * norm_gain
    ).astype(jnp.bfloat16)
    normed_flat = normed.reshape(dialogs * seq_len, width)
    query_cols = w_query.shape[1]
    keyval_cols = w_keyval.shape[2]
    pieces = (
        lax.all_gather(w_query, "dp", axis=0, tiled=True),
        lax.all_gather(w_keyval, "dp", axis=0, tiled=True),
    )
    keyval_piece = pieces[1].reshape(pieces[1].shape[0], 2 * keyval_cols)
    query_sum = jnp.dot(normed_flat, pieces[0], preferred_element_type=jnp.float32)
    keyval_sum = jnp.dot(normed_flat, keyval_piece, preferred_element_type=jnp.float32)
    positions = jnp.arange(seq_len)
    local_heads = query_cols // HEAD_DIM
    local_kv = keyval_cols // HEAD_DIM
    query = jax.vmap(lambda block: rotate(block, positions))(
        query_sum.reshape(dialogs, seq_len, local_heads, HEAD_DIM)
    ).astype(jnp.bfloat16)
    keys = jax.vmap(lambda block: rotate(block, positions))(
        keyval_sum[:, :keyval_cols].reshape(dialogs, seq_len, local_kv, HEAD_DIM)
    ).astype(jnp.bfloat16)
    values = (
        keyval_sum[:, keyval_cols:]
        .reshape(dialogs, seq_len, local_kv, HEAD_DIM)
        .astype(jnp.bfloat16)
    )
    pooled_context = jax.vmap(attend)(query, keys, values, lengths).astype(jnp.bfloat16)
    valid = (positions[None, :] < lengths[:, None]).astype(jnp.float32)
    pooled_input = (
        jnp.sum(hidden * valid[:, :, None], axis=1) / lengths.astype(jnp.float32)[:, None]
    )
    partial_out = jnp.dot(
        pooled_context,
        lax.all_gather(w_out, "dp", axis=1, tiled=True),
        preferred_element_type=jnp.float32,
    )
    projected = lax.psum(partial_out.astype(jnp.bfloat16), "mp").astype(jnp.float32)
    embedding = pooled_input + projected
    unit = embedding * lax.rsqrt(jnp.sum(embedding * embedding, axis=-1, keepdims=True) + 1e-06)
    unit = (unit * flags.astype(jnp.float32)[:, None]).astype(jnp.bfloat16)
    my_index = lax.axis_index("dp")
    owner_count = lax.axis_size("dp")
    my_count = jnp.sum(jnp.where(owner == my_index, counts, 0))
    members = residents[0]
    member_count = members.shape[0]
    inverse_norm = lax.rsqrt(
        jnp.einsum("md,md->m", members, members, preferred_element_type=jnp.float32) + 1e-06
    )
    member_start = lax.axis_index("mp") * member_count
    live = member_start + jnp.arange(member_count) < my_count
    table_size = owner.shape[0]
    cluster_ids = cluster[:, 0]
    destination = jnp.sum(
        jnp.where(jnp.arange(table_size)[None, :] == cluster_ids[:, None], owner[None, :], 0),
        axis=1,
    )
    capacity = max(1, -(-dialogs // owner_count))
    order = jnp.arange(dialogs)
    earlier = (destination[None, :] == destination[:, None]) & (order[None, :] < order[:, None])
    rank = jnp.sum(earlier.astype(jnp.int32), axis=1)
    onehot = (jnp.arange(owner_count)[:, None, None] == destination[None, None, :]) & (
        jnp.arange(capacity)[None, :, None] == rank[None, None, :]
    )
    outgoing = jnp.einsum(
        "ocn,nd->ocd", onehot.astype(jnp.bfloat16), unit, preferred_element_type=jnp.float32
    ).astype(jnp.bfloat16)
    query_rows = lax.all_to_all(outgoing, "dp", split_axis=0, concat_axis=0, tiled=True)
    dots = lax.dot_general(
        query_rows,
        members,
        (((query_rows.ndim - 1,), (1,)), ((), ())),
        preferred_element_type=jnp.float32,
    )
    returned = lax.all_to_all(
        jnp.where(live, logit_scale * dots * inverse_norm, 0.0).astype(jnp.bfloat16),
        "dp",
        split_axis=0,
        concat_axis=0,
        tiled=True,
    ).astype(jnp.float32)
    similarity = jnp.einsum(
        "ocn,ocm->nm", onehot.astype(jnp.float32), returned, precision=lax.Precision.HIGHEST
    )
    return similarity


def solution(mesh):
    in_specs = (
        P("dp", None, "mp"),
        P(),
        P("dp", "mp"),
        P("dp", None, "mp"),
        P("mp", "dp"),
        P("dp", "mp", None),
        P("dp"),
        P("dp", None),
        P(),
        P(),
        P("dp"),
    )
    out_specs = P("dp", "mp")
    return jax.shard_map(local, mesh=mesh, in_specs=in_specs, out_specs=out_specs, check_vma=False)
```

profile of v0, /device:TPU:0, one launch (start us, length us, event | category | flops | bytes accessed | tf_op | source)
XLA Modules:
  0.0 408.5 jit_solution(2310838354348667568)
XLA Ops:
  6.5 0.7 all-gather.9.cloned.1.call-update
  7.3 0.0 all-gather.5.cloned.1.call-start
  7.3 0.7 all-gather.5.cloned.1.call-update
  8.0 0.0 all-gather.7.cloned.1.call-start
  8.1 0.7 all-gather.7.cloned.1.call-update
  8.7 0.0 all-gather.11.cloned.1.call-start
  8.8 0.5 all-gather.11.cloned.1.call-update
  9.3 0.0 all-reduce.2.cloned.1.call-start
  9.4 0.7 convert_element_type.91
  10.0 0.7 convert_element_type.99
  10.7 0.8 select_reduce_fusion
  11.5 0.2 convert_reduce_fusion
  11.7 0.7 iota_compare_fusion.1
  12.4 0.2 multiply_cosine_fusion
  12.6 0.3 broadcast_and_fusion
  12.9 2.8 fusion.6
  15.7 97.3 %all-gather.9.cloned.1.call-done = bf16[3584,896]{1,0:T(8,128)(2,1)} async-done(((bf16[448,896]{1,0:T(8,128)(2,1)}), bf16[3584,896]{1,0:T(8,128)(2,1)}) %all-gather.9.cloned.1.call-update) | async-done | bytes 6422544 | tf_op jit(solution)/shard_map/all_gather | solution.py:59
  113.0 9.7 %copy.20 = bf16[896,3584]{1,0:T(8,128)(2,1)} copy(bf16[896,3584]{0,1:T(8,128)(2,1)} %bitcast.86) | data formatting | bytes 12845056 | tf_op jit(solution)/shard_map/dot_general | solution.py:63
  122.7 63.2 %all-gather.5.cloned.1.call-done = bf16[32,48,3584]{2,1,0:T(8,128)(2,1)} async-done(((bf16[32,48,896]{2,1,0:T(8,128)(2,1)}), bf16[32,48,3584]{2,1,0:T(8,128)(2,1)}) %all-gather.5.cloned.1.call-update) | async-done | bytes 11010064 | tf_op jit(solution)/shard_map/all_gather | solution.py:49
  185.8 8.9 %fusion = (f32[32,3584]{1,0:T(8,128)S(1)}, f32[32,48]{1,0:T(8,128)S(1)}) fusion(bf16[32,48,3584]{2,1,0:T(8,128)(2,1)} %all-gather.5.cloned.1.call-done, f32[32,48]{1,0:T(8,128)S(1)} %get-tuple-element.14), kind=kLoop, calls=%fused_computation.3 | loop fusion | flops 27408896 | bytes 11481088 | tf_op jit(solution)/shard_map/reduce_sum | solution.py:82
  194.8 11.0 %fusion.3 = bf16[32,48,3584]{2,1,0:T(8,128)(2,1)} fusion(bf16[32,48,3584]{2,1,0:T(8,128)(2,1)} %all-gather.5.cloned.1.call-done, f32[3584]{0:T(1024)S(1)} %copy-done.1, f32[32,48]{1,0:T(8,128)S(1)} %add_rsqrt_fusion), kind=kLoop, calls=%fused_computation.6 | loop fusion | flops 22020096 | bytes 22040576 | tf_op jit(solution)/shard_map/convert_element_type | solution.py:54
  205.7 28.8 %all-gather.7.cloned.1.call-done = bf16[3584,2,128]{2,1,0:T(2,128)(2,1)} async-done(((bf16[448,2,128]{2,1,0:T(2,128)(2,1)}), bf16[3584,2,128]{2,1,0:T(2,128)(2,1)}) %all-gather.7.cloned.1.call-update) | async-done | bytes 1835024 | tf_op jit(solution)/shard_map/all_gather | solution.py:60
  234.5 7.2 %fusion.22 = f32[1536,256]{1,0:T(8,128)S(1)} fusion(bf16[1536,3584]{1,0:T(8,128)(2,1)} %bitcast.84, bf16[448,8,2,128]{3,2,1,0:T(2,128)(2,1)} %bitcast.92), kind=kOutput, calls=%fused_computation.34 | convolution fusion | flops 2818572288 | bytes 14417920 | tf_op jit(solution)/shard_map/dot_general | solution.py:64
  241.7 0.1 slice.26
  241.8 0.1 slice.48
  241.8 0.3 fusion.36
  242.2 0.2 copy-done
  242.4 1.5 slice-done.1
  243.8 11.6 %fusion.4 = f32[32,48,7,128]{3,1,2,0:T(8,128)S(1)} fusion(bf16[7,128,3584,1]{2,1,0,3:T(8,128)(2,1)S(1)} %bitcast.89, bf16[32,48,3584]{2,1,0:T(8,128)(2,1)S(1)} %copy-done), kind=kOutput, calls=%fused_computation.7 | convolution fusion | flops 9865003008 | bytes 22937600 | tf_op jit(solution)/shard_map/dot_general | solution.py:63
  255.5 1.9 subtract_convert_fusion
  257.4 3.6 fusion.9
  261.0 2.1 fusion.8
  263.2 2.3 fusion.7
  265.5 0.0 copy-start.2
  265.5 0.0 copy-start.3
  265.5 70.8 %all-gather.11.cloned.1.call-done = bf16[896,3584]{0,1:T(8,128)(2,1)} async-done(((bf16[896,448]{0,1:T(8,128)(2,1)}), bf16[896,3584]{0,1:T(8,128)(2,1)}) %all-gather.11.cloned.1.call-update) | async-done | bytes 6422544 | tf_op jit(solution)/shard_map/all_gather | solution.py:86
  336.3 5.5 %convolution_convert_fusion.1 = bf16[32,3584]{1,0:T(8,128)(2,1)} fusion(bf16[896,3584]{0,1:T(8,128)(2,1)} %all-gather.11.cloned.1.call-done, f32[4,8,7,128]{3,2,1,0:T(8,128)S(1)} %bitcast.91, f32[32]{0:T(128)S(1)} %convert_element_type.91), kind=kOutput, calls=%fused_computation.20 | convolution fusion | flops 205692928 | bytes 6766720 | tf_op jit(solution)/shard_map/dot_general | solution.py:84
  341.8 0.0 all-reduce.2.cloned.1.call-update
  341.8 30.2 %all-reduce.2.cloned.1.call-done = bf16[32,3584]{1,0:T(8,128)(2,1)} async-done(((bf16[32,3584]{1,0:T(8,128)(2,1)}), bf16[32,3584]{1,0:T(8,128)(2,1)}) %all-reduce.2.cloned.1.call-update) | async-done | bytes 229392 | tf_op jit(solution)/shard_map/psum | solution.py:89
  372.0 1.2 multiply_reduce_fusion
  373.2 1.9 convolution_convert_fusion
  375.1 5.5 %all-to-all-start = ((bf16[8,4,3584]{2,1,0:T(4,128)(2,1)}), bf16[8,4,3584]{2,1,0:T(4,128)(2,1)S(1)}, u32[]{:S(2)}, u32[]{:S(2)}) async-start(bf16[8,4,3584]{2,1,0:T(4,128)(2,1)} %convolution_convert_fusion), calls=%async_computation | async-start | bytes 458752 | tf_op jit(solution)/shard_map/all_to_all | solution.py:119
  380.7 0.6 fusion.50
  381.3 0.7 add_compare_fusion
  382.0 6.7 %all-to-all-done = bf16[8,4,3584]{2,1,0:T(4,128)(2,1)S(1)} async-done(((bf16[8,4,3584]{2,1,0:T(4,128)(2,1)}), bf16[8,4,3584]{2,1,0:T(4,128)(2,1)S(1)}, u32[]{:S(2)}, u32[]{:S(2)}) %all-to-all-start) | async-done | bytes 229408 | tf_op jit(solution)/shard_map/all_to_all | solution.py:119
  388.7 3.2 fusion.33
  391.9 9.2 %all_to_all.10 = bf16[8,4,512]{2,1,0:T(4,128)(2,1)S(1)} all-to-all(bf16[8,4,512]{2,1,0:T(4,128)(2,1)S(1)} %fusion.33), channel_id=1, replica_groups=mesh['dp'=8,'mp'=4] {'dp'}, dimensions={0} | all-to-all | bytes 65536 | tf_op jit(solution)/shard_map/all_to_all | solution.py:126
  401.2 0.8 convolution_bitcast_fusion
  (19 shorter events, 0.1 us)
Async XLA Ops:
  6.5 106.4 %all-gather.9.cloned.1.call-start = ((), (), s32[]{:S(2)}) async-start(), calls=%async_computation.4 | async-start | bytes 7225344 | tf_op jit(solution)/shard_map/all_gather | solution.py:59
  7.3 178.6 %all-gather.5.cloned.1.call-start = ((), (), s32[]{:S(2)}) async-start(), calls=%async_computation.2 | async-start | bytes 13762560 | tf_op jit(solution)/shard_map/all_gather | solution.py:49
  8.0 226.5 %all-gather.7.cloned.1.call-start = ((), (), s32[]{:S(2)}) async-start(), calls=%async_computation.3 | async-start | bytes 2064384 | tf_op jit(solution)/shard_map/all_gather | solution.py:60
  8.7 327.5 %all-gather.11.cloned.1.call-start = ((), (), s32[]{:S(2)}) async-start(), calls=%async_computation.5 | async-start | bytes 7225344 | tf_op jit(solution)/shard_map/all_gather | solution.py:86
  9.3 362.7 %all-reduce.2.cloned.1.call-start = ((), (), s32[]{:S(2)}) async-start(), calls=%async_computation.6 | async-start | bytes 458752 | tf_op jit(solution)/shard_map/psum | solution.py:89
  185.8 8.9 %copy-start.1 = (f32[3584]{0:T(1024)S(1)}, f32[3584]{0:T(1024)}, u32[]{:S(2)}) copy-start(f32[3584]{0:T(1024)} %param.12) | copy-start | bytes 43012
  194.8 47.4 %slice-start = ((s8[6422528]{0:T(1024)(128)(4,1)}), s8[2228224]{0:T(1024)(128)(4,1)S(1)}, s32[]{:S(2)}) async-start(s8[6422528]{0:T(1024)(128)(4,1)} %bitcast.87), calls=%async_computation.7 | async-start | bytes 4456448
  234.5 7.8 %copy-start = (bf16[32,48,3584]{2,1,0:T(8,128)(2,1)S(1)}, bf16[32,48,3584]{2,1,0:T(8,128)(2,1)}, u32[]{:S(2)}) copy-start(bf16[32,48,3584]{2,1,0:T(8,128)(2,1)} %fusion.3) | copy-start | bytes 33030148
  234.5 9.3 %slice-start.1 = ((s8[6422528]{0:T(1024)(128)(4,1)}), s8[4194304]{0:T(1024)(128)(4,1)S(1)}, s32[]{:S(2)}) async-start(s8[6422528]{0:T(1024)(128)(4,1)} %bitcast.87), calls=%async_computation.8 | async-start | bytes 8388608
  265.5 115.2 %copy-start.2 = (s32[8]{0:T(128)S(1)}, s32[8]{0:T(128)}, u32[]{:S(2)}) copy-start(s32[8]{0:T(128)} %param.19) | copy-start | bytes 100
  265.5 115.2 %copy-start.3 = (s32[8]{0:T(128)S(1)}, s32[8]{0:T(128)}, u32[]{:S(2)}) copy-start(s32[8]{0:T(128)} %param.20) | copy-start | bytes 100
  375.1 13.5 %all-to-all-start = ((bf16[8,4,3584]{2,1,0:T(4,128)(2,1)}), bf16[8,4,3584]{2,1,0:T(4,128)(2,1)S(1)}, u32[]{:S(2)}, u32[]{:S(2)}) async-start(bf16[8,4,3584]{2,1,0:T(4,128)(2,1)} %convolution_convert_fusion), calls=%async_computation | async-start | bytes 458752 | tf_op jit(solution)/shard_map/all_to_all | solution.py:119
Sparse Core Ops, SparseCore 0:
  9.5 103.3 all-gather.8
  114.5 71.2 all-gather.4
  188.0 46.4 all-gather.6
  236.6 99.6 all-gather.10
  341.9 30.0 all-reduce.1
where the time goes:
time: 409 us
  waiting for transfers between devices  299 us (73%)
  matrix products  36.3 us (9%)
  other arithmetic  33 us (8%)
  between operations  13.3 us (3%)
  local copies, waits for them, and re-layouts  11.5 us (3%)
  blocking collectives  9.24 us (2%)
  starting transfers between devices  5.66 us (1%)
    all_gather x1, waiting for transfers between devices, local(): lax.all_gather(w_query, 'dp', axis=0, tiled=True)  97.3 us
    all_gather x1, waiting for transfers between devices, local(): lax.all_gather(w_out, 'dp', axis=1, tiled=True)  70.8 us
    all_gather x1, waiting for transfers between devices, local(): gathered = lax.all_gather(tokens, 'mp', axis=2, tiled=True)  63.2 us
    psum x1, waiting for transfers between devices, local(): lax.psum(partial_out.astype(jnp.bfloat16), 'mp').astype(jnp.float32)  30.2 us
    all_gather x1, waiting for transfers between devices, local(): lax.all_gather(w_keyval, 'dp', axis=0, tiled=True)  28.8 us
    dot_general x1, matrix products, local(): jnp.dot(normed_flat, pieces[0], preferred_element_type=jnp.float32)  11.6 us
    convert_element_type x1, other arithmetic, local(): normed = (hidden * lax.rsqrt(jnp.mean(hidden * hidden, axis=-1, keepdims=...  11 us
    dot_general x1, local copies, waits for them, and re-layouts, local(): jnp.dot(normed_flat, pieces[0], preferred_element_type=jnp.float32)  9.72 us
  transfers between devices with their start and end apart: 6, of which 6 were waited for; matrix products, arithmetic and copies ran while one was open for 16% of the time, Pallas kernels for 0%

commit v1 on v0

--- a/solution.py
+++ b/solution.py
@@ -46,7 +46,12 @@
 def local(
     tokens, norm_gain, w_query, w_keyval, w_out, residents, lengths, cluster, owner, counts, flags
 ):
-    gathered = lax.all_gather(tokens, "mp", axis=2, tiled=True)
+    ring = [tokens]
+    for hop in range(3):
+        ring.append(lax.ppermute(ring[-1], "mp", [(dev, (dev + 1) % 4) for dev in range(4)]))
+    gathered = jnp.roll(
+        jnp.concatenate(ring[::-1], axis=2), (lax.axis_index("mp") + 1) * ring[0].shape[2], axis=2
+    )
     dialogs, seq_len, width = gathered.shape
     hidden = gathered.astype(jnp.float32)
     normed = (

time: 409 us -> 335 us (0.82)
  waiting for transfers between devices: 299 us -> 190 us
  local copies, waits for them, and re-layouts: 11.5 us -> 31.9 us
  other arithmetic: 33 us -> 42.9 us
    all_gather x1, waiting for transfers between devices: 97.3 us -> 0.02 us  [local(): lax.all_gather(w_query, 'dp', axis=0, tiled=True)]
    ppermute x0 -> x3, waiting for transfers between devices: none -> 91.8 us  [local(): lax.ppermute(ring[-1], 'mp', [(dev, (dev + 1) % 4) for dev in range(4)])]
    all_gather x1 -> x0, waiting for transfers between devices: 63.2 us -> none  [local(): gathered = lax.all_gather(tokens, 'mp', axis=2, tiled=True)]
    all_gather x1, waiting for transfers between devices: 28.8 us -> 0.01 us  [local(): lax.all_gather(w_keyval, 'dp', axis=0, tiled=True)]
    unnamed x12 -> x15, local copies, waits for them, and re-layouts: 1.67 us -> 20.3 us
    all_gather x1, waiting for transfers between devices: 70.8 us -> 60 us  [local(): lax.all_gather(w_out, 'dp', axis=1, tiled=True)]
    reduce_sum x1, other arithmetic: 8.89 us -> 17.1 us  [local(): jnp.sum(hidden * valid[:, :, None], axis=1)]
    dot_general x1, matrix products: 11.6 us -> 16.2 us  [local(): jnp.dot(normed_flat, pieces[0], preferred_element_type=jnp.float32)]
  transfers between devices with their start and end apart: 6 -> 8, of which waited for: 6 -> 6; matrix products, arithmetic and copies ran while one was open for 16% -> 31% of each run, Pallas kernels for 0% -> 0%
where the time goes in v1:
time: 335 us; the launch traced here: 334 us
  waiting for transfers between devices  190 us (57%)
  other arithmetic  42.9 us (13%)
  matrix products  40.1 us (12%)
  local copies, waits for them, and re-layouts  31.9 us (10%)
  between operations  13.3 us (4%)
  blocking collectives  9.24 us (3%)
  starting transfers between devices  6.18 us (2%)
    ppermute x3, waiting for transfers between devices, local(): lax.ppermute(ring[-1], 'mp', [(dev, (dev + 1) % 4) for dev in range(4)])  91.8 us
    all_gather x1, waiting for transfers between devices, local(): lax.all_gather(w_out, 'dp', axis=1, tiled=True)  60 us
    psum x1, waiting for transfers between devices, local(): lax.psum(partial_out.astype(jnp.bfloat16), 'mp').astype(jnp.float32)  30.2 us
    unnamed x15, local copies, waits for them, and re-layouts  20.3 us
    reduce_sum x1, other arithmetic, local(): jnp.sum(hidden * valid[:, :, None], axis=1)  17.1 us
    dot_general x1, matrix products, local(): jnp.dot(normed_flat, pieces[0], preferred_element_type=jnp.float32)  16.2 us
    convert_element_type x1, other arithmetic, local(): normed = (hidden * lax.rsqrt(jnp.mean(hidden * hidden, axis=-1, keepdims=...  12.6 us
    dot_general x1, local copies, waits for them, and re-layouts, local(): jnp.dot(normed_flat, pieces[0], preferred_element_type=jnp.float32)  9.71 us
  transfers between devices with their start and end apart: 8, of which 6 were waited for; matrix products, arithmetic and copies ran while one was open for 31% of the time, Pallas kernels for 0%

profile of v1, /device:TPU:0, one launch (start us, length us, event | category | flops | bytes accessed | tf_op | source)
XLA Modules:
  0.0 333.7 jit_solution(12209955997691914518)
XLA Ops:
  6.5 0.7 all-gather.4.cloned.1.call-update
  7.3 0.7 all-gather.6.cloned.1.call-update
  8.1 0.5 collective-permute-start
  8.6 32.9 %collective-permute-done = bf16[32,48,896]{2,1,0:T(8,128)(2,1)S(1)} collective-permute-done((bf16[32,48,896]{2,1,0:T(8,128)(2,1)}, bf16[32,48,896]{2,1,0:T(8,128)(2,1)S(1)}, u32[]{:S(2)}, u32[]{:S(2)}) %collective-permute-start) | collective-permute-done | bytes 2752544 | tf_op jit(solution)/shard_map/ppermute | solution.py:51
  41.5 0.0 collective-permute-start.1
  41.5 32.5 %collective-permute-done.1 = bf16[32,48,896]{2,1,0:T(8,128)(2,1)} collective-permute-done((bf16[32,48,896]{2,1,0:T(8,128)(2,1)S(1)}, bf16[32,48,896]{2,1,0:T(8,128)(2,1)}, u32[]{:S(2)}, u32[]{:S(2)}) %collective-permute-start.1) | collective-permute-done | bytes 2752544 | tf_op jit(solution)/shard_map/ppermute | solution.py:51
  74.1 0.0 all-reduce.2.cloned.1.call-start
  74.2 0.7 convert_element_type.91
  74.8 0.7 convert_element_type.99
  75.5 0.8 select_reduce_fusion
  76.2 0.2 convert_reduce_fusion
  76.5 0.7 iota_compare_fusion.1
  77.2 0.2 multiply_cosine_fusion
  77.4 0.3 broadcast_and_fusion
  77.6 2.9 fusion.6
  80.5 26.4 %collective-permute-done.2 = bf16[32,48,896]{2,1,0:T(8,128)(2,1)} collective-permute-done((bf16[32,48,896]{2,1,0:T(8,128)(2,1)}, bf16[32,48,896]{2,1,0:T(8,128)(2,1)}, u32[]{:S(2)}, u32[]{:S(2)}) %collective-permute-start.2) | collective-permute-done | bytes 2752544 | tf_op jit(solution)/shard_map/ppermute | solution.py:51
  106.8 3.6 %constant_dynamic-update-slice_fusion.7 = bf16[32,48,7168]{2,1,0:T(8,128)(2,1)} fusion(bf16[32,48,896]{2,1,0:T(8,128)(2,1)} %collective-permute-done.2), kind=kLoop, calls=%fused_computation.70 | loop fusion | bytes 5505024
  110.4 3.9 %constant_dynamic-update-slice_fusion.6 = bf16[32,48,7168]{2,1,0:T(8,128)(2,1)} fusion(bf16[32,48,7168]{2,1,0:T(8,128)(2,1)} %constant_dynamic-update-slice_fusion.7, bf16[32,48,896]{2,1,0:T(8,128)(2,1)} %collective-permute-done.1), kind=kLoop, calls=%fused_computation.69 | loop fusion | bytes 5505024
  114.3 1.8 constant_dynamic-update-slice_fusion.5
  116.2 1.9 constant_dynamic-update-slice_fusion.4
  118.0 3.6 %constant_dynamic-update-slice_fusion.3 = bf16[32,48,7168]{2,1,0:T(8,128)(2,1)} fusion(bf16[32,48,7168]{2,1,0:T(8,128)(2,1)} %constant_dynamic-update-slice_fusion.4, bf16[32,48,896]{2,1,0:T(8,128)(2,1)} %collective-permute-done.2), kind=kLoop, calls=%fused_computation.66 | loop fusion | bytes 5505024
  121.7 3.6 %constant_dynamic-update-slice_fusion.2 = bf16[32,48,7168]{2,1,0:T(8,128)(2,1)} fusion(bf16[32,48,7168]{2,1,0:T(8,128)(2,1)} %constant_dynamic-update-slice_fusion.3, bf16[32,48,896]{2,1,0:T(8,128)(2,1)} %collective-permute-done.1), kind=kLoop, calls=%fused_computation.65 | loop fusion | bytes 5505024
  125.3 1.8 constant_dynamic-update-slice_fusion.1
  127.1 1.8 constant_dynamic-update-slice_fusion
  128.9 17.1 %fusion = (f32[32,3584]{1,0:T(8,128)S(1)}, f32[32,48]{1,0:T(8,128)S(1)}) fusion(f32[32,48]{1,0:T(8,128)S(1)} %get-tuple-element.14, bf16[32,48,7168]{2,1,0:T(8,128)(2,1)} %constant_dynamic-update-slice_fusion, s32[]{:T(128)S(6)} %select_n.32), kind=kLoop, calls=%fused_computation.3 | loop fusion | flops 27408896 | bytes 11481092 | tf_op jit(solution)/shard_map/reduce_sum | solution.py:87
  146.0 12.6 %fusion.3 = bf16[32,48,3584]{2,1,0:T(8,128)(2,1)} fusion(f32[3584]{0:T(1024)S(1)} %copy-done.1, f32[32,48]{1,0:T(8,128)S(1)} %add_rsqrt_fusion, bf16[32,48,7168]{2,1,0:T(8,128)(2,1)} %constant_dynamic-update-slice_fusion, s32[]{:T(128)S(6)} %select_n.32), kind=kLoop, calls=%fused_computation.6 | loop fusion | flops 22020096 | bytes 22040580 | tf_op jit(solution)/shard_map/convert_element_type | solution.py:59
  158.6 6.3 %fusion.22 = f32[1536,256]{1,0:T(8,128)S(1)} fusion(bf16[1536,3584]{1,0:T(8,128)(2,1)} %bitcast.84, bf16[448,8,2,128]{3,2,1,0:T(2,128)(2,1)} %bitcast.90), kind=kOutput, calls=%fused_computation.34 | convolution fusion | flops 2818572288 | bytes 14417920 | tf_op jit(solution)/shard_map/dot_general | solution.py:69
  165.0 0.1 slice.26
  165.0 0.1 slice.48
  165.1 0.3 fusion.36
  165.5 9.7 %copy.20 = bf16[896,3584]{1,0:T(8,128)(2,1)} copy(bf16[896,3584]{0,1:T(8,128)(2,1)} %bitcast.86) | data formatting | bytes 12845056 | tf_op jit(solution)/shard_map/dot_general | solution.py:68
  175.2 16.2 %fusion.4 = f32[32,48,7,128]{3,1,2,0:T(8,128)S(1)} fusion(bf16[7,128,3584,1]{2,1,0,3:T(8,128)(2,1)} %bitcast.87, bf16[32,48,3584]{2,1,0:T(8,128)(2,1)} %fusion.3), kind=kOutput, calls=%fused_computation.7 | convolution fusion | flops 9865003008 | bytes 22937600 | tf_op jit(solution)/shard_map/dot_general | solution.py:68
  191.4 1.9 subtract_convert_fusion
  193.4 3.4 %fusion.9 = (f32[32,7,48]{2,1,0:T(8,128)S(1)}, f32[32,48,48,7]{2,1,3,0:T(8,128)S(1)}) fusion(pred[32,48,48]{1,2,0:T(8,128)(4,1)S(1)} %broadcast_and_fusion, bf16[32,48,7,64]{3,1,2,0:T(8,128)(2,1)S(1)} %get-tuple-element.8, bf16[32,48,7,64]{3,1,2,0:T(8,128)(2,1)S(1)} %get-tuple-element.7, bf16[32,48,64]{2,1,0:T(8,128)(2,1)S(1)} %get-tuple-element.10, ...), kind=kOutput, calls=%fused_computation.21 | convolution fusion | flops 139949568 | bytes 5326848 | tf_op jit(solution)/shard_map/vmap(qkgd,pkd->kgqp)/dot_general | solution.py:30
  196.8 2.1 fusion.8
  198.9 2.5 fusion.7
  201.5 60.0 %all-gather.8.cloned.1.call-done = bf16[896,3584]{0,1:T(8,128)(2,1)} async-done(((bf16[896,448]{0,1:T(8,128)(2,1)}), bf16[896,3584]{0,1:T(8,128)(2,1)}) %all-gather.8.cloned.1.call-update) | async-done | bytes 6422544 | tf_op jit(solution)/shard_map/all_gather | solution.py:91
  261.4 5.5 %convolution_convert_fusion.1 = bf16[32,3584]{1,0:T(8,128)(2,1)} fusion(bf16[896,3584]{0,1:T(8,128)(2,1)} %all-gather.8.cloned.1.call-done, f32[4,8,7,128]{3,2,1,0:T(8,128)S(1)} %bitcast.89, f32[32]{0:T(128)S(1)} %convert_element_type.91), kind=kOutput, calls=%fused_computation.20 | convolution fusion | flops 205692928 | bytes 6766720 | tf_op jit(solution)/shard_map/dot_general | solution.py:89
  267.0 30.2 %all-reduce.2.cloned.1.call-done = bf16[32,3584]{1,0:T(8,128)(2,1)} async-done(((bf16[32,3584]{1,0:T(8,128)(2,1)}), bf16[32,3584]{1,0:T(8,128)(2,1)}) %all-reduce.2.cloned.1.call-update) | async-done | bytes 229392 | tf_op jit(solution)/shard_map/psum | solution.py:94
  297.2 1.2 multiply_reduce_fusion
  298.4 1.9 convolution_convert_fusion
  300.3 5.5 %all-to-all-start = ((bf16[8,4,3584]{2,1,0:T(4,128)(2,1)}), bf16[8,4,3584]{2,1,0:T(4,128)(2,1)S(1)}, u32[]{:S(2)}, u32[]{:S(2)}) async-start(bf16[8,4,3584]{2,1,0:T(4,128)(2,1)} %convolution_convert_fusion), calls=%async_computation | async-start | bytes 458752 | tf_op jit(solution)/shard_map/all_to_all | solution.py:124
  305.8 0.6 fusion.50
  306.5 0.7 add_compare_fusion
  307.1 6.7 %all-to-all-done = bf16[8,4,3584]{2,1,0:T(4,128)(2,1)S(1)} async-done(((bf16[8,4,3584]{2,1,0:T(4,128)(2,1)}), bf16[8,4,3584]{2,1,0:T(4,128)(2,1)S(1)}, u32[]{:S(2)}, u32[]{:S(2)}) %all-to-all-start) | async-done | bytes 229408 | tf_op jit(solution)/shard_map/all_to_all | solution.py:124
  313.8 3.2 fusion.33
  317.1 9.2 %all_to_all.10 = bf16[8,4,512]{2,1,0:T(4,128)(2,1)S(1)} all-to-all(bf16[8,4,512]{2,1,0:T(4,128)(2,1)S(1)} %fusion.33), channel_id=1, replica_groups=mesh['dp'=8,'mp'=4] {'dp'}, dimensions={0} | all-to-all | bytes 65536 | tf_op jit(solution)/shard_map/all_to_all | solution.py:131
  326.3 0.8 convolution_bitcast_fusion
  (25 shorter events, 0.2 us)
Async XLA Ops:
  6.5 152.1 %all-gather.4.cloned.1.call-start = ((), (), s32[]{:S(2)}) async-start(), calls=%async_computation.2 | async-start | bytes 2064384 | tf_op jit(solution)/shard_map/all_gather | solution.py:65
  7.3 158.2 %all-gather.6.cloned.1.call-start = ((), (), s32[]{:S(2)}) async-start(), calls=%async_computation.3 | async-start | bytes 7225344 | tf_op jit(solution)/shard_map/all_gather | solution.py:64
  8.0 253.4 %all-gather.8.cloned.1.call-start = ((), (), s32[]{:S(2)}) async-start(), calls=%async_computation.4 | async-start | bytes 7225344 | tf_op jit(solution)/shard_map/all_gather | solution.py:91
  8.1 33.4 %collective-permute-start = (bf16[32,48,896]{2,1,0:T(8,128)(2,1)}, bf16[32,48,896]{2,1,0:T(8,128)(2,1)S(1)}, u32[]{:S(2)}, u32[]{:S(2)}) collective-permute-start(bf16[32,48,896]{2,1,0:T(8,128)(2,1)} %param.11), channel_id=1, source_target_pairs={{0,1},{1,2},{2,3},{3,0},{4,5},{5,6},{6,7},{7,4},{8,9},{9,10},{10,1... | collective-permute-start | bytes 8257544 | tf_op jit(solution)/shard_map/ppermute | solution.py:51
  41.5 32.6 %collective-permute-start.1 = (bf16[32,48,896]{2,1,0:T(8,128)(2,1)S(1)}, bf16[32,48,896]{2,1,0:T(8,128)(2,1)}, u32[]{:S(2)}, u32[]{:S(2)}) collective-permute-start(bf16[32,48,896]{2,1,0:T(8,128)(2,1)S(1)} %collective-permute-done), channel_id=1, source_target_pairs={{0,1},{1,2},{2,3},{3,0},{4,5},{5,6},{6,7},{7,4},{8,9},{9,10},{10,1... | collective-permute-start | bytes 8257544 | tf_op jit(solution)/shard_map/ppermute | solution.py:51
  74.1 32.8 %collective-permute-start.2 = (bf16[32,48,896]{2,1,0:T(8,128)(2,1)}, bf16[32,48,896]{2,1,0:T(8,128)(2,1)}, u32[]{:S(2)}, u32[]{:S(2)}) collective-permute-start(bf16[32,48,896]{2,1,0:T(8,128)(2,1)} %collective-permute-done.1), channel_id=1, source_target_pairs={{0,1},{1,2},{2,3},{3,0},{4,5},{5,6},{6,7},{7,4},{8,9},{9,10},{10,1... | collective-permute-start | bytes 8257544 | tf_op jit(solution)/shard_map/ppermute | solution.py:51
  74.1 223.1 %all-reduce.2.cloned.1.call-start = ((), (), s32[]{:S(2)}) async-start(), calls=%async_computation.5 | async-start | bytes 458752 | tf_op jit(solution)/shard_map/psum | solution.py:94
  110.4 5.7 %copy-start = (bf16[32,48,896]{2,1,0:T(8,128)(2,1)S(1)}, bf16[32,48,896]{2,1,0:T(8,128)(2,1)}, u32[]{:S(2)}) copy-start(bf16[32,48,896]{2,1,0:T(8,128)(2,1)} %param.11) | copy-start | bytes 8257540
  128.9 17.1 %copy-start.1 = (f32[3584]{0:T(1024)S(1)}, f32[3584]{0:T(1024)}, u32[]{:S(2)}) copy-start(f32[3584]{0:T(1024)} %param.12) | copy-start | bytes 43012
  201.4 104.4 %copy-start.2 = (s32[8]{0:T(128)S(1)}, s32[8]{0:T(128)}, u32[]{:S(2)}) copy-start(s32[8]{0:T(128)} %param.19) | copy-start | bytes 100
  201.4 104.4 %copy-start.3 = (s32[8]{0:T(128)S(1)}, s32[8]{0:T(128)}, u32[]{:S(2)}) copy-start(s32[8]{0:T(128)} %param.20) | copy-start | bytes 100
  300.3 13.5 %all-to-all-start = ((bf16[8,4,3584]{2,1,0:T(4,128)(2,1)}), bf16[8,4,3584]{2,1,0:T(4,128)(2,1)S(1)}, u32[]{:S(2)}, u32[]{:S(2)}) async-start(bf16[8,4,3584]{2,1,0:T(4,128)(2,1)} %convolution_convert_fusion), calls=%async_computation | async-start | bytes 458752 | tf_op jit(solution)/shard_map/all_to_all | solution.py:124
Sparse Core Ops, SparseCore 0:
  9.5 48.9 all-gather.3
  60.7 99.6 all-gather.5
  162.6 98.8 all-gather.7
  267.1 30.0 all-reduce.1
